TPU v7x, 256 devices: a whole 4x4x8 slice. The times are simulated.
256 devices in a mesh: front: 32 (over y, x, core), row: 8 (over z).
Axes of the slice: x: 4, y: 4, z: 8, core: 2. Of those that a mesh axis runs over, the one named last changes fastest.
Arguments:
- rhs_front: bfloat16 [65536, 384], P(('front', 'row')), may hold values from -6 to 6
- rhs_root: float32 [12288, 384], P('row'), may hold values from -6 to 6
- pivot_inverse: bfloat16 [65536, 2048], P(('front', 'row')), may hold values from -0.125 to 0.125
- border_coupling: bfloat16 [196608, 2048], P(('front', 'row')), may hold values from -0.125 to 0.125
- root_inverse: bfloat16 [12288, 12288], P('front', 'row'), may hold values from -0.0546875 to 0.0546875
- border_map: int32 [32, 48], P('front', 'row'), may hold values from 0 to 95, as said below
Outputs:
- front_solution: float32 [65536, 384], P(('front', 'row'))
- root_solution: float32 [12288, 384], P(('front', 'row'))
Inputs may be any that keep to these rules, and one draw needn't show every extreme that they name: `border_map`: for each front and each index r of row, the 6 border blocks held at that index name distinct root blocks, all among blocks r * 12 to (r + 1) * 12 - 1; a root block may be named by many fronts or by none.
All inputs are finite; a program needn't handle non-finite values.
Results may differ from a plain program's by a relative error of at most 0.0075.
Values may be sent and summed in bfloat16 or wider, within the bound.
A program may use at most 64 MiB of HBM per device.

v0:
```python
import jax
import jax.numpy as jnp
from jax import lax
from jax.sharding import PartitionSpec as P

BLK = 128


def per_device(rhs_front, rhs_root, pivot_inverse, border_coupling, root_inverse, border_map):
    row_at = lax.axis_index("row")
    width = rhs_front.shape[1]

    def pivot_step(piece):
        return jnp.dot(pivot_inverse, piece, preferred_element_type=jnp.float32)

    inner = pivot_step(lax.all_gather(rhs_front, "row", axis=0, tiled=True))
    inner_half = inner.astype(jnp.bfloat16)
    columns = border_coupling
    contrib = jnp.dot(
        columns,
        lax.all_gather(inner_half, "row", axis=0, tiled=True),
        preferred_element_type=jnp.float32,
    )
    block_local = border_map.shape[1]
    span_rows = root_inverse.shape[1]
    span_blocks = span_rows // BLK
    local_index = border_map[0] - row_at * span_blocks
    select = (local_index[None, :] == jnp.arange(span_blocks, dtype=jnp.int32)[:, None]).astype(
        jnp.float32
    )
    dense = jnp.einsum(
        "kj,jcn->kcn",
        select,
        contrib.reshape(block_local, BLK, width),
        precision=lax.Precision.HIGHEST,
    ).reshape(span_rows, width)
    schur_rhs = (rhs_root - lax.psum(dense, "front")).astype(jnp.bfloat16)
    root_solution = lax.psum_scatter(
        jnp.dot(root_inverse, schur_rhs, preferred_element_type=jnp.float32),
        "row",
        scatter_dimension=0,
        tiled=True,
    )
    root_half = root_solution.astype(jnp.bfloat16)
    gathered = lax.all_gather(root_half, ("front", "row"), axis=0, tiled=True)
    ranged = lax.dynamic_slice_in_dim(gathered, row_at * span_rows, span_rows, 0)
    picked = jnp.einsum(
        "kj,kcn->jcn",
        select.astype(jnp.bfloat16),
        ranged.reshape(span_blocks, BLK, width),
        preferred_element_type=jnp.float32,
    )
    picked = picked.astype(jnp.bfloat16).reshape(block_local * BLK, width)
    columns = border_coupling
    pulled = lax.psum_scatter(
        lax.dot_general(
            columns, picked, (((0,), (0,)), ((), ())), preferred_element_type=jnp.float32
        ),
        "row",
        scatter_dimension=0,
        tiled=True,
    ).astype(jnp.bfloat16)
    correction = pivot_step(lax.all_gather(pulled, "row", axis=0, tiled=True))
    return (inner - correction, root_solution)


def solution(mesh):
    in_specs = (
        P(("front", "row"), None),
        P("row", None),
        P(("front", "row"), None),
        P(("front", "row"), None),
        P("front", "row"),
        P("front", "row"),
    )
    out_specs = (P(("front", "row"), None), P(("front", "row"), None))
    return jax.shard_map(
        per_device, mesh=mesh, in_specs=in_specs, out_specs=out_specs, check_vma=False
    )
```

profile of v0, /device:TPU:2, one launch (start us, length us, event | category | flops | bytes accessed | tf_op | source)
XLA Modules:
  0.0 491.7 jit_solution(16187609789959951527)
XLA Ops:
  7.2 0.0 copy-start
  7.2 0.0 all-gather.5.cloned.1.call-start
  7.2 0.7 all-gather.5.cloned.1.call-update
  7.9 0.0 copy-start.1
  7.9 0.0 all-gather.7.cloned.1.call-start
  8.0 44.3 %all-gather.5.cloned.1.call-done = bf16[2048,384]{1,0:T(8,128)(2,1)} async-done(((bf16[256,384]{1,0:T(8,128)(2,1)}), bf16[2048,384]{1,0:T(8,128)(2,1)}) %all-gather.5.cloned.1.call-update) | async-done | bytes 1572880 | tf_op jit(solution)/shard_map/all_gather | solution.py:16
  52.3 3.1 fusion.14
  55.4 0.0 all-gather.7.cloned.1.call-update
  55.4 0.0 all-reduce.2.cloned.1.call-start
  55.5 0.0 copy-done.1
  55.5 38.2 %all-gather.7.cloned.1.call-done = bf16[2048,384]{1,0:T(8,128)(2,1)} async-done(((bf16[256,384]{1,0:T(8,128)(2,1)}), bf16[2048,384]{1,0:T(8,128)(2,1)}) %all-gather.7.cloned.1.call-update) | async-done | bytes 1572880 | tf_op jit(solution)/shard_map/all_gather | solution.py:21
  93.7 0.0 copy-done
  93.7 3.9 convolution_bitcast_fusion.1
  97.6 2.7 copy.27
  100.3 3.5 fusion.2
  103.7 2.1 copy.29
  105.9 0.0 all-reduce.2.cloned.1.call-update
  105.9 0.0 reduce-scatter.7.cloned.1.call-start
  105.9 115.6 %all-reduce.2.cloned.1.call-done = f32[1536,384]{1,0:T(8,128)} async-done(((f32[1536,384]{1,0:T(8,128)}), f32[1536,384]{1,0:T(8,128)}) %all-reduce.2.cloned.1.call-update) | async-done | bytes 2359312 | tf_op jit(solution)/shard_map/psum | solution.py:37
  221.6 4.3 convolution_bitcast_fusion.2
  225.9 2.1 copy.36
  228.0 0.0 reduce-scatter.7.cloned.1.call-update
  228.0 0.0 all-gather.9.cloned.1.call-start
  228.1 38.4 %reduce-scatter.7.cloned.1.call-done = f32[48,384]{1,0:T(8,128)} async-done(((f32[384,384]{1,0:T(8,128)}), f32[48,384]{1,0:T(8,128)}) %reduce-scatter.7.cloned.1.call-update) | async-done | bytes 73744 | tf_op jit(solution)/shard_map/reduce_scatter | solution.py:38
  266.5 1.5 convert_element_type.25
  268.0 0.0 all-gather.9.cloned.1.call-update
  268.0 0.0 reduce-scatter.5.cloned.1.call-start
  268.1 119.6 %all-gather.9.cloned.1.call-done = bf16[12288,384]{1,0:T(8,128)(2,1)} async-done(((bf16[48,384]{1,0:T(8,128)(2,1)}), bf16[12288,384]{1,0:T(8,128)(2,1)}) %all-gather.9.cloned.1.call-update) | async-done | bytes 9437200 | tf_op jit(solution)/shard_map/all_gather | solution.py:45
  387.7 1.4 constant_dynamic-slice_fusion
  389.1 0.8 fusion.4
  389.9 0.1 copy.32
  390.0 3.1 convolution_bitcast_fusion
  393.1 0.0 reduce-scatter.5.cloned.1.call-update
  393.1 0.0 all-gather.11.cloned.1.call-start
  393.1 43.8 %reduce-scatter.5.cloned.1.call-done = f32[256,384]{0,1:T(8,128)} async-done(((f32[2048,384]{0,1:T(8,128)}), f32[256,384]{0,1:T(8,128)}) %reduce-scatter.5.cloned.1.call-update) | async-done | bytes 393232 | tf_op jit(solution)/shard_map/reduce_scatter | solution.py:55
  436.9 1.7 convert_element_type.27
  438.6 0.0 all-gather.11.cloned.1.call-update
  438.7 43.1 %all-gather.11.cloned.1.call-done = bf16[2048,384]{0,1:T(8,128)(2,1)} async-done(((bf16[256,384]{0,1:T(8,128)(2,1)}), bf16[2048,384]{0,1:T(8,128)(2,1)}) %all-gather.11.cloned.1.call-update) | async-done | bytes 1572880 | tf_op jit(solution)/shard_map/all_gather | solution.py:63
  481.7 3.2 fusion.7
  (1 shorter events, 0.0 us)
Async XLA Ops:
  7.2 86.6 %copy-start = (bf16[768,2048]{1,0:T(8,128)(2,1)S(1)}, bf16[768,2048]{1,0:T(8,128)(2,1)}, u32[]{:S(2)}) copy-start(bf16[768,2048]{1,0:T(8,128)(2,1)} %param.9) | copy-start | bytes 9437188
  7.2 45.1 %all-gather.5.cloned.1.call-start = ((), (), s32[]{:S(2)}) async-start(), calls=%async_computation.2 | async-start | bytes 1769472 | tf_op jit(solution)/shard_map/all_gather | solution.py:16
  7.9 47.6 %copy-start.1 = (s32[1,6]{1,0:T(1,128)S(1)}, s32[1,6]{1,0:T(1,128)}, u32[]{:S(2)}) copy-start(s32[1,6]{1,0:T(1,128)} %param.11) | copy-start | bytes 76
  7.9 85.8 %all-gather.7.cloned.1.call-start = ((), (), s32[]{:S(2)}) async-start(), calls=%async_computation.3 | async-start | bytes 1769472 | tf_op jit(solution)/shard_map/all_gather | solution.py:21
  55.4 166.1 %all-reduce.2.cloned.1.call-start = ((), (), s32[]{:S(2)}) async-start(), calls=%async_computation.4 | async-start | bytes 4718592 | tf_op jit(solution)/shard_map/psum | solution.py:37
  105.9 160.6 %reduce-scatter.7.cloned.1.call-start = ((), (), s32[]{:S(2)}) async-start(), calls=%async_computation.8 | async-start | bytes 663552 | tf_op jit(solution)/shard_map/reduce_scatter | solution.py:38
  228.0 159.7 %all-gather.9.cloned.1.call-start = ((), (), s32[]{:S(2)}) async-start(), calls=%async_computation.5 | async-start | bytes 9474048 | tf_op jit(solution)/shard_map/all_gather | solution.py:45
  268.0 168.9 %reduce-scatter.5.cloned.1.call-start = ((), (), s32[]{:S(2)}) async-start(), calls=%async_computation.6 | async-start | bytes 3538944 | tf_op jit(solution)/shard_map/reduce_scatter | solution.py:55
  393.1 88.7 %all-gather.11.cloned.1.call-start = ((), (), s32[]{:S(2)}) async-start(), calls=%async_computation.7 | async-start | bytes 1769472 | tf_op jit(solution)/shard_map/all_gather | solution.py:63
Sparse Core Ops, SparseCore 0:
  9.8 42.4 all-gather.4
  55.6 38.1 all-gather.6
  106.0 115.5 all-reduce.1
  228.2 38.3 reduce-scatter.6
  270.8 116.9 all-gather.8
  393.2 43.6 reduce-scatter.4
  439.2 42.4 all-gather.10
where the time goes:
time: 492 us
  waiting for transfers between devices  444 us (90%)
  matrix products  21.8 us (4%)
  between operations  14.2 us (3%)
  local copies, waits for them, and re-layouts  8.41 us (2%)
    all_gather x1, waiting for transfers between devices, per_device(): gathered = lax.all_gather(root_half, ('front', 'row'), axis=0, tiled=True)  120 us
    psum x1, waiting for transfers between devices, per_device(): schur_rhs = (rhs_root - lax.psum(dense, 'front')).astype(jnp.bfloat16)  116 us
    all_gather x1, waiting for transfers between devices, per_device(): inner = pivot_step(lax.all_gather(rhs_front, 'row', axis=0, tiled=True))  44.3 us
    reduce_scatter x1, waiting for transfers between devices, per_device(): lax.psum_scatter(lax.dot_general(columns, picked, (((0,), (0,)), ((), ())...  43.8 us
    all_gather x1, waiting for transfers between devices, per_device(): correction = pivot_step(lax.all_gather(pulled, 'row', axis=0, tiled=True))  43.1 us
    reduce_scatter x1, waiting for transfers between devices, per_device(): lax.psum_scatter(jnp.dot(root_inverse, schur_rhs, preferred_element_type=...  38.4 us
    all_gather x1, waiting for transfers between devices, per_device(): lax.all_gather(inner_half, 'row', axis=0, tiled=True)  38.2 us
  transfers between devices with their start and end apart: 7, of which 7 were waited for; matrix products, arithmetic and copies ran while one was open for 0% of the time, Pallas kernels for 0%

commit v1 on v0

v1 whole, which is shorter than its diff:
```python
import functools

import jax
import jax.numpy as jnp
from jax import lax
from jax.experimental import pallas as pl
from jax.experimental.pallas import tpu as pltpu
from jax.sharding import PartitionSpec as P

BLK = 128
NX, NY, NZ = 4, 4, 8
PIECE = 48
CHUNKS = ((0, 128), (128, 128), (256, 128))
F32, BF16 = jnp.float32, jnp.bfloat16
N_COPIES = 80


def scratch_for(w):
    v = pltpu.VMEM
    return dict(
        g1=v((NZ, 256, w), BF16),
        inner=v((256, w), F32),
        g2=v((NZ, 256, w), BF16),
        contrib=v((6, BLK, w), F32),
        s0=v((6, BLK, w), F32),
        r0=v((6, BLK, w), F32),
        dense=v((768, w), F32),
        sx=v((2, 2, 192, w), F32),
        rx=v((2, 2, 192, w), F32),
        ey=v((192, w), F32),
        sy=v((2, 2, PIECE, w), F32),
        ry=v((2, 2, PIECE, w), F32),
        h=v((1536, w), BF16),
        part=v((384, w), F32),
        sz=v((2, 4, PIECE, w), F32),
        rz=v((2, 4, PIECE, w), F32),
        t=v((PIECE, w), BF16),
        k=v((1536, w), BF16),
        picked=v((768, w), BF16),
        q=v((NZ, w, 256), F32),
        sp=v((2, 4, w, 256), BF16),
        rp=v((2, 4, w, 256), BF16),
        g3=v((NZ, w, 256), BF16),
    )


NAMES = tuple(scratch_for(128))


def mod(a, n):
    return lax.rem(a + 2 * n, n)


def kernel(rhs, rroot, pinv, coup, rinv, bmap, out_f, out_r, *scratch):
    per = len(NAMES)
    bufs = [
        dict(zip(NAMES, scratch[i * per : (i + 1) * per])) for i in range(len(CHUNKS))
    ]
    pinv_v, coup_v, rinv_v, root_v, send_sems, recv_sems, load_sems = scratch[per * len(CHUNKS) :]

    f = lax.axis_index("front")
    z = lax.axis_index("row")
    c = lax.rem(f, 2)
    x = lax.rem(lax.div(f, 2), NX)
    y = lax.div(f, 2 * NX)

    def dev(x_, y_, c_, z_):
        return ((y_ * NX + x_) * 2 + c_, z_)

    rings = {
        "z": (NZ, z, dev(x, y, c, mod(z + 1, NZ)), dev(x, y, c, mod(z - 1, NZ))),
        "x": (NX, x, dev(mod(x + 1, NX), y, c, z), dev(mod(x - 1, NX), y, c, z)),
        "y": (NY, y, dev(x, mod(y + 1, NY), c, z), dev(x, mod(y - 1, NY), c, z)),
    }
    other = dev(x, y, 1 - c, z)
    perm_to = dev(
        mod(x + 2 * lax.div(z, 4), NX), mod(y + z, NY), 1 - c, 2 * y + lax.div(x, 2)
    )
    piece_out = (2 * lax.rem(x, 2) + c) * NZ + z
    y0 = lax.div(z, 2)
    x0 = 2 * lax.rem(z, 2)
    core_from = 1 - c

    def group_of(x_at):
        d = mod(x_at - x0, NX)
        return (2 * lax.rem(d, 2) + core_from) * NZ + 4 * lax.div(d, 2)

    def low_of(y_at):
        return mod(y_at - y0, NY)

    d_me = mod(x - x0, NX)
    perm_from = dev(
        x0 + lax.rem(d_me, 2), y0, core_from, 4 * lax.div(d_me, 2) + low_of(y)
    )

    loads = {}

    def load(name, src, dst):
        copy = pltpu.make_async_copy(src, dst, load_sems.at[len(loads)])
        copy.start()
        loads[name] = [copy, False]

    def need(name):
        entry = loads[name]
        if not entry[1]:
            entry[0].wait()
            entry[1] = True

    barrier = pltpu.get_barrier_semaphore()
    partners = [other, perm_to, perm_from]
    for _, _, plus, minus in rings.values():
        partners += [plus, minus]
    for partner in partners:
        pl.semaphore_signal(
            barrier, inc=1, device_id=partner, device_id_type=pl.DeviceIdType.MESH
        )
    piece_row = pl.multiple_of(((c * NX + x) * NY + y) * PIECE, 8)
    for i, (c0, w) in enumerate(CHUNKS):
        load(f"own{i}", rhs.at[:, pl.ds(c0, w)], bufs[i]["g1"].at[z])
    load("pinv", pinv, pinv_v)
    load("coup", coup, coup_v)
    load("root", rroot.at[pl.ds(piece_row, PIECE), :], root_v)
    load("rinv", rinv, rinv_v)
    pl.semaphore_wait(barrier, len(partners))

    starts = []

    def chunk(i, c0, w):
        b = bufs[i]
        count = [0]
        own_copies = []

        def send(src, dst, to):
            at = count[0]
            count[0] += 1
            copy = pltpu.make_async_remote_copy(
                src_ref=src,
                dst_ref=dst,
                send_sem=send_sems.at[i, at],
                recv_sem=recv_sems.at[i, at],
                device_id=to,
                device_id_type=pl.DeviceIdType.MESH,
            )
            copy.start()
            own_copies.append(copy)
            return copy

        def gather(axis, slot, split, first=None):
            n, me, plus, minus = rings[axis]
            half = n // 2
            src = slot(me) if first is None else first
            a = send(src, slot(me), plus)
            d = send(src, slot(me), minus)
            for s in range(1, half):
                yield
                a.wait_recv()
                got = slot(mod(me - s, n))
                if s == half - 1:
                    got = split(got, 0)
                a = send(got, got, plus)
                d.wait_recv()
                got = slot(mod(me + s, n))
                if s == half - 1:
                    got = split(got, 1)
                d = send(got, got, minus)
            yield
            a.wait_recv()
            d.wait_recv()

        def scatter(axis, own, rows, cut, sbuf, rbuf, wire):
            n, me, plus, minus = rings[axis]
            half = n // 2
            far = own(mod(me + half, n))
            sides = ((slice(0, cut), plus), (slice(cut, rows), minus))
            copies = []
            for side, (span, to) in enumerate(sides):
                sbuf[side, 0, span, :] = far[span, :].astype(wire)
                copies.append(
                    send(sbuf.at[side, 0, span, :], rbuf.at[side, 0, span, :], to)
                )
            for s in range(1, half):
                yield
                for side, (span, to) in enumerate(sides):
                    copies[side].wait_recv()
                    at = mod(me + half - s, n) if side == 0 else mod(me - half + s, n)
                    mine = own(at)
                    if s == 1:
                        rest = slice(cut, rows) if side == 0 else slice(0, cut)
                        sbuf[side, 1, span, :] = (
                            mine[span, :] + rbuf[side, 0, span, :].astype(F32)
                        ).astype(wire)
                        sbuf[side, 1, rest, :] = mine[rest, :].astype(wire)
                    else:
                        sbuf[side, s] = (mine[...] + rbuf[side, s - 1].astype(F32)).astype(wire)
                    copies[side] = send(sbuf.at[side, s], rbuf.at[side, s], to)
            yield
            copies[0].wait_recv()
            copies[1].wait_recv()
            if half == 1:
                raise ValueError
            return (
                own(me)[...]
                + rbuf[0, half - 1].astype(F32)
                + rbuf[1, half - 1].astype(F32)
            )

        def halves(cut, rows):
            def split(ref, side):
                return ref.at[pl.ds(0, cut), :] if side == 0 else ref.at[pl.ds(cut, rows - cut), :]

            return split

        def rows_of(ref, start, size):
            return ref.at[pl.ds(pl.multiple_of(start, 16), size), :]

        yield from gather(
            "z", lambda at: b["g1"].at[at], halves(128, 256), first=rhs.at[:, pl.ds(c0, w)]
        )
        need(f"own{i}")
        need("pinv")
        inner = jnp.dot(
            pinv_v[...], b["g1"][...].reshape(2048, w), preferred_element_type=F32
        )
        b["inner"][...] = inner
        b["g2"][z] = inner.astype(BF16)
        yield from gather("z", lambda at: b["g2"].at[at], halves(128, 256))
        need("coup")
        b["contrib"][...] = jnp.dot(
            coup_v[...], b["g2"][...].reshape(2048, w), preferred_element_type=F32
        ).reshape(6, BLK, w)
        local = [bmap[0, j] - z * 12 for j in range(6)]

        def placed(block):
            total = b["contrib"][0] * (local[0] == block).astype(F32)
            for j in range(1, 6):
                total = total + b["contrib"][j] * (local[j] == block).astype(F32)
            return total

        for j in range(6):
            b["s0"][j] = placed((1 - c) * 6 + j)
        swap = send(b["s0"], b["r0"], other)
        for j in range(6):
            b["dense"][j * BLK : (j + 1) * BLK, :] = placed(c * 6 + j)
        yield
        swap.wait_recv()
        b["dense"][...] = b["dense"][...] + b["r0"][...].reshape(768, w)
        b["ey"][...] = yield from scatter(
            "x",
            lambda at: rows_of(b["dense"], at * 192, 192),
            192,
            96,
            b["sx"],
            b["rx"],
            F32,
        )
        total = yield from scatter(
            "y", lambda at: rows_of(b["ey"], at * PIECE, PIECE), PIECE, 24, b["sy"], b["ry"], F32
        )
        need("root")
        h_at = (c * NX + x) * NY
        rows_of(b["h"], (h_at + y) * PIECE, PIECE)[...] = (
            root_v[:, c0 : c0 + w] - total
        ).astype(BF16)
        yield from gather(
            "y", lambda at: rows_of(b["h"], (h_at + at) * PIECE, PIECE), halves(32, PIECE)
        )
        yield from gather(
            "x", lambda at: rows_of(b["h"], (c * NX + at) * 192, 192), halves(96, 192)
        )
        mine = rows_of(b["h"], c * 768, 768)
        swap = send(mine, mine, other)
        yield
        swap.wait_recv()
        need("rinv")
        b["part"][...] = jnp.dot(rinv_v[...], b["h"][...], preferred_element_type=F32)
        root = yield from scatter(
            "z",
            lambda at: rows_of(b["part"], at * PIECE, PIECE),
            PIECE,
            24,
            b["sz"],
            b["rz"],
            F32,
        )
        out_r[:, c0 : c0 + w] = root
        b["t"][...] = root.astype(BF16)
        moved = send(b["t"], rows_of(b["k"], piece_out * PIECE, PIECE), perm_to)
        yield
        moved.wait_recv()
        k_at = group_of(x)
        yield from gather(
            "y",
            lambda at: rows_of(b["k"], (k_at + low_of(at)) * PIECE, PIECE),
            halves(32, PIECE),
        )
        yield from gather(
            "x", lambda at: rows_of(b["k"], group_of(at) * PIECE, 192), halves(96, 192)
        )
        swaps = []
        for g in range(2):
            mine = rows_of(b["k"], (g * 16 + core_from * 8) * PIECE, 8 * PIECE)
            swaps.append(send(mine, mine, other))
        yield
        for swap in swaps:
            swap.wait_recv()
        for j in range(6):
            total = b["k"][0:BLK, :] * (local[j] == 0).astype(F32).astype(BF16)
            for at in range(1, 12):
                mask = (local[j] == at).astype(F32).astype(BF16)
                total = total + b["k"][at * BLK : (at + 1) * BLK, :] * mask
            b["picked"][j * BLK : (j + 1) * BLK, :] = total
        pulled = lax.dot_general(
            b["picked"][...],
            coup_v[...],
            (((0,), (0,)), ((), ())),
            preferred_element_type=F32,
        )
        for at in range(NZ):
            b["q"][at] = pulled[:, at * 256 : (at + 1) * 256]
        total = yield from scatter(
            "z", lambda at: b["q"].at[at], w, w // 2, b["sp"], b["rp"], BF16
        )
        b["g3"][z] = total.astype(BF16)
        yield from gather("z", lambda at: b["g3"].at[at], halves(w // 2, w))
        result = b["inner"][...]
        for at in range(NZ):
            result = result - lax.dot_general(
                pinv_v[:, at * 256 : (at + 1) * 256],
                b["g3"][at],
                (((1,), (1,)), ((), ())),
                preferred_element_type=F32,
            )
        out_f[:, c0 : c0 + w] = result
        for copy in own_copies:
            copy.wait_send()

    live = [chunk(i, c0, w) for i, (c0, w) in enumerate(CHUNKS)]
    while live:
        for gen in list(live):
            try:
                next(gen)
            except StopIteration:
                live.remove(gen)


def per_device(*args):
    scratch = []
    for _, w in CHUNKS:
        scratch += list(scratch_for(w).values())
    scratch += [
        pltpu.VMEM((256, 2048), BF16),
        pltpu.VMEM((768, 2048), BF16),
        pltpu.VMEM((384, 1536), BF16),
        pltpu.VMEM((PIECE, 384), F32),
        pltpu.SemaphoreType.DMA((len(CHUNKS), N_COPIES)),
        pltpu.SemaphoreType.DMA((len(CHUNKS), N_COPIES)),
        pltpu.SemaphoreType.DMA((8,)),
    ]
    hbm = pl.BlockSpec(memory_space=pl.ANY)
    vmem = pl.BlockSpec(memory_space=pltpu.VMEM)
    return pl.pallas_call(
        kernel,
        out_shape=(
            jax.ShapeDtypeStruct((256, 384), F32),
            jax.ShapeDtypeStruct((PIECE, 384), F32),
        ),
        in_specs=[hbm] * 5 + [pl.BlockSpec(memory_space=pltpu.SMEM)],
        out_specs=(vmem, vmem),
        scratch_shapes=scratch,
        compiler_params=pltpu.CompilerParams(
            collective_id=0, has_side_effects=True, vmem_limit_bytes=60 * 2**20
        ),
        name="solve",
    )(*args)


def solution(mesh):
    in_specs = (
        P(("front", "row"), None),
        P("row", None),
        P(("front", "row"), None),
        P(("front", "row"), None),
        P("front", "row"),
        P("front", "row"),
    )
    out_specs = (P(("front", "row"), None), P(("front", "row"), None))
    return jax.shard_map(
        per_device, mesh=mesh, in_specs=in_specs, out_specs=out_specs, check_vma=False
    )
```

time: 492 us -> 157 us (0.32)
  waiting for transfers between devices: 444 us -> 0 us
  Pallas kernels: 0 us -> 153 us
  matrix products: 21.8 us -> 0 us
  between operations: 14.2 us -> 0.64 us
  local copies, waits for them, and re-layouts: 8.41 us -> 3.29 us
    all_gather x4 -> x0, waiting for transfers between devices: 245 us -> none  [the longest x1 120 us: per_device(): gathered = lax.all_gather(root_half, ('front', 'row'), axis=0, tiled=True)]
    pallas_call x0 -> x1, Pallas kernels: none -> 153 us  [per_device(): pl.pallas_call(kernel, out_shape=(jax.ShapeDtypeStruct((256, 384), F32),...]
    psum x1 -> x0, waiting for transfers between devices: 116 us -> none  [per_device(): schur_rhs = (rhs_root - lax.psum(dense, 'front')).astype(jnp.bfloat16)]
    reduce_scatter x2 -> x0, waiting for transfers between devices: 82.2 us -> none  [the longest x1 43.8 us: per_device(): lax.psum_scatter(lax.dot_general(columns, picked, (((0,), (0,)), ((), ())...]
    dot_general x7 -> x0, matrix products: 21.8 us -> none  [the longest x2 6.29 us: pivot_step(): return jnp.dot(pivot_inverse, piece, preferred_element_type=jnp.float32)]
  transfers between devices with their start and end apart: 7 -> 0, of which waited for: 7 -> 0; matrix products, arithmetic and copies ran while one was open for 0% -> 0% of each run, Pallas kernels for 0% -> 0%
where the time goes in v1:
time: 157 us
  Pallas kernels  153 us (97%)
  local copies, waits for them, and re-layouts  3.29 us (2%)
    pallas_call x1, Pallas kernels, per_device(): pl.pallas_call(kernel, out_shape=(jax.ShapeDtypeStruct((256, 384), F32),...  153 us
    unnamed x2, local copies, waits for them, and re-layouts  3.29 us

profile of v1, /device:TPU:2, one launch (start us, length us, event | category | flops | bytes accessed | tf_op | source)
XLA Modules:
  0.0 157.1 jit_solution(7356377604763340569)
XLA Ops:
  0.6 153.2 %solve.1 = (f32[256,384]{1,0:T(8,128)}, f32[48,384]{1,0:T(8,128)}) custom-call(bf16[256,384]{1,0:T(8,128)(2,1)} %rhs.1, f32[1536,384]{1,0:T(8,128)} %rroot.1, bf16[256,2048]{1,0:T(8,128)(2,1)} %pinv.1, bf16[768,2048]{1,0:T(8,128)(2,1)} %coup.1, bf16[384,1536]{1,0:T(8,128)(2,1)} %rinv.1, s32[1,6]{1,0:T(1,128)} %bmap.1), custom_call_target="tpu_custom_call" | custom-call | tf_op jit(solution)/shard_map/solve/pallas_call | solution.py:361
  153.8 1.8 %copy.10 = f32[256,384]{1,0:T(8,128)} copy(f32[256,384]{1,0:T(8,128)} %get-tuple-element.4) | data formatting | bytes 786432
  155.6 1.5 copy.11

commit v2 on v1

--- a/solution.py
+++ b/solution.py
@@ -12,7 +12,11 @@
 PIECE = 48
 CHUNKS = ((0, 128), (128, 128), (256, 128))
 F32, BF16 = jnp.float32, jnp.bfloat16
-N_COPIES = 80
+OFFSETS = sorted(
+    ((dx, dy) for dx in range(NX) for dy in range(NY) if dx or dy),
+    key=lambda o: -(min(o[0], NX - o[0]) + min(o[1], NY - o[1])),
+)
+N_COPIES = 112
 
 
 def scratch_for(w):
@@ -25,15 +29,12 @@
         s0=v((6, BLK, w), F32),
         r0=v((6, BLK, w), F32),
         dense=v((768, w), F32),
-        sx=v((2, 2, 192, w), F32),
-        rx=v((2, 2, 192, w), F32),
-        ey=v((192, w), F32),
-        sy=v((2, 2, PIECE, w), F32),
-        ry=v((2, 2, PIECE, w), F32),
+        sxy=v((768, w), BF16),
+        rxy=v((16, PIECE, w), BF16),
         h=v((1536, w), BF16),
         part=v((384, w), F32),
-        sz=v((2, 4, PIECE, w), F32),
-        rz=v((2, 4, PIECE, w), F32),
+        parth=v((384, w), BF16),
+        r5=v((NZ, PIECE, w), BF16),
         t=v((PIECE, w), BF16),
         k=v((1536, w), BF16),
         picked=v((768, w), BF16),
@@ -56,7 +57,7 @@
     bufs = [
         dict(zip(NAMES, scratch[i * per : (i + 1) * per])) for i in range(len(CHUNKS))
     ]
-    pinv_v, coup_v, rinv_v, root_v, send_sems, recv_sems, load_sems = scratch[per * len(CHUNKS) :]
+    pinv_v, coup_v, rinv_v, root_v, send_sems, recv_sems, load_sems, pass_sems = scratch[per * len(CHUNKS) :]
 
     f = lax.axis_index("front")
     z = lax.axis_index("row")
@@ -88,11 +89,6 @@
     def low_of(y_at):
         return mod(y_at - y0, NY)
 
-    d_me = mod(x - x0, NX)
-    perm_from = dev(
-        x0 + lax.rem(d_me, 2), y0, core_from, 4 * lax.div(d_me, 2) + low_of(y)
-    )
-
     loads = {}
 
     def load(name, src, dst):
@@ -107,7 +103,7 @@
             entry[1] = True
 
     barrier = pltpu.get_barrier_semaphore()
-    partners = [other, perm_to, perm_from]
+    partners = [other]
     for _, _, plus, minus in rings.values():
         partners += [plus, minus]
     for partner in partners:
@@ -123,15 +119,30 @@
     load("rinv", rinv, rinv_v)
     pl.semaphore_wait(barrier, len(partners))
 
-    starts = []
+    def passing():
+        for r in range(3):
+            for axis in "xy":
+                for to in rings[axis][2:]:
+                    pl.semaphore_signal(
+                        pass_sems.at[r], inc=1, device_id=to, device_id_type=pl.DeviceIdType.MESH
+                    )
+            yield
+            pl.semaphore_wait(pass_sems.at[r], 4)
+
+    passes = passing()
+    all_copies = []
+
+    def in_plane():
+        for _ in passes:
+            pass
 
     def chunk(i, c0, w):
         b = bufs[i]
         count = [0]
-        own_copies = []
 
         def send(src, dst, to):
             at = count[0]
+            assert at < N_COPIES
             count[0] += 1
             copy = pltpu.make_async_remote_copy(
                 src_ref=src,
@@ -142,7 +153,7 @@
                 device_id_type=pl.DeviceIdType.MESH,
             )
             copy.start()
-            own_copies.append(copy)
+            all_copies.append(copy)
             return copy
 
         def gather(axis, slot, split, first=None):
@@ -204,6 +215,13 @@
                 + rbuf[1, half - 1].astype(F32)
             )
 
+        def to_plane(src_of, dst_of):
+            copies = []
+            for dx, dy in OFFSETS:
+                to = (mod(x + dx, NX), mod(y + dy, NY))
+                copies.append(send(src_of(*to), dst_of(dx, dy), dev(*to, c, z)))
+            return copies
+
         def halves(cut, rows):
             def split(ref, side):
                 return ref.at[pl.ds(0, cut), :] if side == 0 else ref.at[pl.ds(cut, rows - cut), :]
@@ -244,58 +262,63 @@
         yield
         swap.wait_recv()
         b["dense"][...] = b["dense"][...] + b["r0"][...].reshape(768, w)
-        b["ey"][...] = yield from scatter(
-            "x",
-            lambda at: rows_of(b["dense"], at * 192, 192),
-            192,
-            96,
-            b["sx"],
-            b["rx"],
-            F32,
-        )
-        total = yield from scatter(
-            "y", lambda at: rows_of(b["ey"], at * PIECE, PIECE), PIECE, 24, b["sy"], b["ry"], F32
-        )
+        b["sxy"][...] = b["dense"][...].astype(BF16)
+        in_plane()
+        mine = (x * NY + y) * PIECE
+        copies = to_plane(
+            lambda x_, y_: rows_of(b["sxy"], (x_ * NY + y_) * PIECE, PIECE),
+            lambda dx, dy: b["rxy"].at[dx * NY + dy],
+        )
+        yield
+        total = rows_of(b["dense"], mine, PIECE)[...]
+        for (dx, dy), copy in zip(OFFSETS, copies):
+            copy.wait_recv()
+            total = total + b["rxy"][dx * NY + dy].astype(F32)
         need("root")
-        h_at = (c * NX + x) * NY
-        rows_of(b["h"], (h_at + y) * PIECE, PIECE)[...] = (
-            root_v[:, c0 : c0 + w] - total
-        ).astype(BF16)
-        yield from gather(
-            "y", lambda at: rows_of(b["h"], (h_at + at) * PIECE, PIECE), halves(32, PIECE)
-        )
-        yield from gather(
-            "x", lambda at: rows_of(b["h"], (c * NX + at) * 192, 192), halves(96, 192)
-        )
+        piece = rows_of(b["h"], c * 768 + mine, PIECE)
+        piece[...] = (root_v[:, c0 : c0 + w] - total).astype(BF16)
+        copies = to_plane(lambda x_, y_: piece, lambda dx, dy: piece)
+        yield
+        for copy in copies:
+            copy.wait_recv()
         mine = rows_of(b["h"], c * 768, 768)
         swap = send(mine, mine, other)
+        need("rinv")
+
+        def root_half(core):
+            cols = pl.ds(pl.multiple_of(core * 768, 256), 768)
+            return jnp.dot(
+                rinv_v[:, cols], rows_of(b["h"], core * 768, 768)[...], preferred_element_type=F32
+            )
+
+        b["part"][...] = root_half(c)
         yield
         swap.wait_recv()
-        need("rinv")
-        b["part"][...] = jnp.dot(rinv_v[...], b["h"][...], preferred_element_type=F32)
-        root = yield from scatter(
-            "z",
-            lambda at: rows_of(b["part"], at * PIECE, PIECE),
-            PIECE,
-            24,
-            b["sz"],
-            b["rz"],
-            F32,
-        )
-        out_r[:, c0 : c0 + w] = root
-        b["t"][...] = root.astype(BF16)
+        part = b["part"][...] + root_half(1 - c)
+        b["part"][...] = part
+        b["parth"][...] = part.astype(BF16)
+        copies = []
+        for s in (4, 3, 5, 2, 6, 1, 7):
+            at = mod(z + s, NZ)
+            copies.append(
+                send(rows_of(b["parth"], at * PIECE, PIECE), b["r5"].at[s], dev(x, y, c, at))
+            )
+        yield
+        total = rows_of(b["part"], z * PIECE, PIECE)[...]
+        for copy in copies:
+            copy.wait_recv()
+        for s in range(1, NZ):
+            total = total + b["r5"][s].astype(F32)
+        out_r[:, c0 : c0 + w] = total
+        b["t"][...] = total.astype(BF16)
         moved = send(b["t"], rows_of(b["k"], piece_out * PIECE, PIECE), perm_to)
         yield
         moved.wait_recv()
-        k_at = group_of(x)
-        yield from gather(
-            "y",
-            lambda at: rows_of(b["k"], (k_at + low_of(at)) * PIECE, PIECE),
-            halves(32, PIECE),
-        )
-        yield from gather(
-            "x", lambda at: rows_of(b["k"], group_of(at) * PIECE, 192), halves(96, 192)
-        )
+        piece = rows_of(b["k"], (group_of(x) + low_of(y)) * PIECE, PIECE)
+        copies = to_plane(lambda x_, y_: piece, lambda dx, dy: piece)
+        yield
+        for copy in copies:
+            copy.wait_recv()
         swaps = []
         for g in range(2):
             mine = rows_of(b["k"], (g * 16 + core_from * 8) * PIECE, 8 * PIECE)
@@ -331,8 +354,6 @@
                 preferred_element_type=F32,
             )
         out_f[:, c0 : c0 + w] = result
-        for copy in own_copies:
-            copy.wait_send()
 
     live = [chunk(i, c0, w) for i, (c0, w) in enumerate(CHUNKS)]
     while live:
@@ -341,6 +362,8 @@
                 next(gen)
             except StopIteration:
                 live.remove(gen)
+    for copy in all_copies:
+        copy.wait_send()
 
 
 def per_device(*args):
@@ -355,6 +378,7 @@
         pltpu.SemaphoreType.DMA((len(CHUNKS), N_COPIES)),
         pltpu.SemaphoreType.DMA((len(CHUNKS), N_COPIES)),
         pltpu.SemaphoreType.DMA((8,)),
+        pltpu.SemaphoreType.REGULAR((3,)),
     ]
     hbm = pl.BlockSpec(memory_space=pl.ANY)
     vmem = pl.BlockSpec(memory_space=pltpu.VMEM)

time: 157 us -> 134 us (0.85)
  Pallas kernels: 153 us -> 130 us
    pallas_call x1, Pallas kernels: 153 us -> 130 us  [per_device(): pl.pallas_call(kernel, out_shape=(jax.ShapeDtypeStruct((256, 384), F32),...]
where the time goes in v2:
time: 134 us
  Pallas kernels  130 us (97%)
  local copies, waits for them, and re-layouts  3.29 us (2%)
    pallas_call x1, Pallas kernels, per_device(): pl.pallas_call(kernel, out_shape=(jax.ShapeDtypeStruct((256, 384), F32),...  130 us
    unnamed x2, local copies, waits for them, and re-layouts  3.29 us

profile of v2, /device:TPU:2, one launch (start us, length us, event | category | flops | bytes accessed | tf_op | source)
XLA Modules:
  0.0 133.7 jit_solution(6728158691094705214)
XLA Ops:
  0.6 129.8 %solve.1 = (f32[256,384]{1,0:T(8,128)}, f32[48,384]{1,0:T(8,128)}) custom-call(bf16[256,384]{1,0:T(8,128)(2,1)} %rhs.1, f32[1536,384]{1,0:T(8,128)} %rroot.1, bf16[256,2048]{1,0:T(8,128)(2,1)} %pinv.1, bf16[768,2048]{1,0:T(8,128)(2,1)} %coup.1, bf16[384,1536]{1,0:T(8,128)(2,1)} %rinv.1, s32[1,6]{1,0:T(1,128)} %bmap.1), custom_call_target="tpu_custom_call" | custom-call | tf_op jit(solution)/shard_map/solve/pallas_call | solution.py:385
  130.4 1.8 %copy.10 = f32[256,384]{1,0:T(8,128)} copy(f32[256,384]{1,0:T(8,128)} %get-tuple-element.4) | data formatting | bytes 786432
  132.2 1.5 %copy.11 = f32[48,384]{1,0:T(8,128)} copy(f32[48,384]{1,0:T(8,128)} %get-tuple-element.5) | data formatting | bytes 147456

commit v3 on v2

v3 whole, which is shorter than its diff:
```python
import functools

import jax
import jax.numpy as jnp
from jax import lax
from jax.experimental import pallas as pl
from jax.experimental.pallas import tpu as pltpu
from jax.sharding import PartitionSpec as P

BLK = 128
NX, NY, NZ = 4, 4, 8
PIECE = 48
CHUNKS = ((0, 128), (128, 128), (256, 128))
F32, BF16 = jnp.float32, jnp.bfloat16
OFFSETS = sorted(
    ((dx, dy) for dx in range(NX) for dy in range(NY) if dx or dy),
    key=lambda o: -(min(o[0], NX - o[0]) + min(o[1], NY - o[1])),
)
N_SEMS = 28


def scratch_for(w):
    v = pltpu.VMEM
    return dict(
        g1=v((NZ, 256, w), BF16),
        inner=v((256, w), F32),
        g2=v((NZ, 256, w), BF16),
        contrib=v((6, BLK, w), F32),
        s0=v((6, BLK, w), BF16),
        r0=v((6, BLK, w), BF16),
        dense=v((768, w), F32),
        sxy=v((768, w), BF16),
        rxy=v((16, PIECE, w), BF16),
        h=v((1536, w), BF16),
        part=v((384, w), F32),
        parth=v((384, w), BF16),
        r5=v((NZ, PIECE, w), BF16),
        t=v((PIECE, w), BF16),
        k=v((1536, w), BF16),
        picked=v((768, w), BF16),
        q=v((NZ, w, 256), F32),
        sp=v((2, 4, w, 256), BF16),
        rp=v((2, 4, w, 256), BF16),
        g3=v((NZ, w, 256), BF16),
        rout=v((PIECE, w), F32),
        fout=v((256, w), F32),
    )


NAMES = tuple(scratch_for(128))


def mod(a, n):
    return lax.rem(a + 2 * n, n)


def kernel(rhs, rroot, pinv, coup, rinv, bmap, out_f, out_r, *scratch):
    per = len(NAMES)
    bufs = [
        dict(zip(NAMES, scratch[i * per : (i + 1) * per])) for i in range(len(CHUNKS))
    ]
    rhs_v, pinv_v, coup_v, rinv_v, root_v, sems, load_sems, store_sems, pass_sems = scratch[per * len(CHUNKS) :]

    f = lax.axis_index("front")
    z = lax.axis_index("row")
    c = lax.rem(f, 2)
    x = lax.rem(lax.div(f, 2), NX)
    y = lax.div(f, 2 * NX)

    def dev(x_, y_, c_, z_):
        return ((y_ * NX + x_) * 2 + c_, z_)

    rings = {
        "z": (NZ, z, dev(x, y, c, mod(z + 1, NZ)), dev(x, y, c, mod(z - 1, NZ))),
        "x": (NX, x, dev(mod(x + 1, NX), y, c, z), dev(mod(x - 1, NX), y, c, z)),
        "y": (NY, y, dev(x, mod(y + 1, NY), c, z), dev(x, mod(y - 1, NY), c, z)),
    }
    other = dev(x, y, 1 - c, z)
    plane_to = 2 * y + lax.div(x, 2)
    u = mod(z - plane_to, NZ)
    h = 1 - lax.div(lax.rem(u + 1, NZ), 4)
    q = lax.rem(12 - u - 2 * h, NY)
    perm_to = dev(
        mod(x + h * (2 * lax.rem(x, 2) - 1), NX), mod(y + q, NY), 1 - c, plane_to
    )
    piece_out = (2 * lax.rem(x, 2) + c) * NZ + z
    core_from = 1 - c
    d = mod(x - 2 * lax.rem(z, 2), NX)
    h_from = lax.div(d, 2)
    q_from = mod(y - lax.div(z, 2), NY)
    u_from = lax.rem(3 + 4 * h_from + lax.rem(5 + 2 * h_from - q_from, NY), NZ)
    piece_in = (2 * lax.rem(lax.div(d + 1, 2), 2) + core_from) * NZ + lax.rem(z + u_from, NZ)

    loads = {}

    def load(name, src, dst):
        copy = pltpu.make_async_copy(src, dst, load_sems.at[len(loads)])
        copy.start()
        loads[name] = [copy, False]

    def need(name):
        entry = loads[name]
        if not entry[1]:
            entry[0].wait()
            entry[1] = True

    barrier = pltpu.get_barrier_semaphore()
    partners = [other]
    for _, _, plus, minus in rings.values():
        partners += [plus, minus]
    for partner in partners:
        pl.semaphore_signal(
            barrier, inc=1, device_id=partner, device_id_type=pl.DeviceIdType.MESH
        )
    piece_row = pl.multiple_of(((c * NX + x) * NY + y) * PIECE, 8)
    load("rhs", rhs, rhs_v)
    load("pinv", pinv, pinv_v)
    load("coup", coup, coup_v)
    load("root", rroot.at[pl.ds(piece_row, PIECE), :], root_v)
    load("rinv", rinv, rinv_v)
    need("rhs")
    for i, (c0, w) in enumerate(CHUNKS):
        bufs[i]["g1"][z] = rhs_v[:, c0 : c0 + w]
    pl.semaphore_wait(barrier, len(partners))

    def passing():
        for r in range(3):
            for axis in "xy":
                for to in rings[axis][2:]:
                    pl.semaphore_signal(
                        pass_sems.at[r], inc=1, device_id=to, device_id_type=pl.DeviceIdType.MESH
                    )
            yield
            pl.semaphore_wait(pass_sems.at[r], 4)

    passes = passing()
    all_sent = []
    stores = []

    def store(src, dst):
        copy = pltpu.make_async_copy(src, dst, store_sems.at[len(stores)])
        copy.start()
        stores.append(copy)


    def in_plane():
        for _ in passes:
            pass

    def chunk(i, c0, w):
        b = bufs[i]
        count = [0]

        def sem():
            at = count[0]
            count[0] += 1
            assert at < N_SEMS
            return sems.at[i, at]

        ring_sems = [[sem() for _ in range(4)] for _ in range(2)]

        def send(src, dst, to, out, into):
            copy = pltpu.make_async_remote_copy(
                src_ref=src,
                dst_ref=dst,
                send_sem=out,
                recv_sem=into,
                device_id=to,
                device_id_type=pl.DeviceIdType.MESH,
            )
            copy.start()
            return copy

        def sent(out, ref):
            all_sent.append((out, ref))

        def arrive(into, ref):
            pltpu.make_async_copy(ref, ref, into).wait()

        def gather(axis, slot, split, seven):
            n, me, plus, minus = rings[axis]
            half = n // 2
            out = sem()
            sent(out, seven)
            ups, downs = ring_sems
            a = send(slot(me), slot(me), plus, out, ups[0])
            d = send(slot(me), slot(me), minus, out, downs[0])
            for s in range(1, half):
                yield
                a.wait_recv()
                got = slot(mod(me - s, n))
                if s == half - 1:
                    got = split(got, 0)
                a = send(got, got, plus, out, ups[s])
                d.wait_recv()
                got = slot(mod(me + s, n))
                if s == half - 1:
                    got = split(got, 1)
                d = send(got, got, minus, out, downs[s])
            yield
            a.wait_recv()
            d.wait_recv()

        def scatter(axis, own, rows, cut, sbuf, rbuf, wire, seven):
            n, me, plus, minus = rings[axis]
            half = n // 2
            far = own(mod(me + half, n))
            sides = ((slice(0, cut), plus), (slice(cut, rows), minus))
            copies = []
            out = sem()
            sent(out, seven)
            for side, (span, to) in enumerate(sides):
                sbuf[side, 0, span, :] = far[span, :].astype(wire)
                copies.append(
                    send(
                        sbuf.at[side, 0, span, :],
                        rbuf.at[side, 0, span, :],
                        to,
                        out,
                        ring_sems[side][0],
                    )
                )
            for s in range(1, half):
                yield
                for side, (span, to) in enumerate(sides):
                    copies[side].wait_recv()
                    at = mod(me + half - s, n) if side == 0 else mod(me - half + s, n)
                    mine = own(at)
                    if s == 1:
                        rest = slice(cut, rows) if side == 0 else slice(0, cut)
                        sbuf[side, 1, span, :] = (
                            mine[span, :] + rbuf[side, 0, span, :].astype(F32)
                        ).astype(wire)
                        sbuf[side, 1, rest, :] = mine[rest, :].astype(wire)
                    else:
                        sbuf[side, s] = (mine[...] + rbuf[side, s - 1].astype(F32)).astype(wire)
                    copies[side] = send(
                        sbuf.at[side, s], rbuf.at[side, s], to, out, ring_sems[side][s]
                    )
            yield
            copies[0].wait_recv()
            copies[1].wait_recv()
            return (
                own(me)[...]
                + rbuf[0, half - 1].astype(F32)
                + rbuf[1, half - 1].astype(F32)
            )

        def to_plane(src_of, dst_of, fifteen):
            out, into = sem(), sem()
            for dx, dy in OFFSETS:
                to = (mod(x + dx, NX), mod(y + dy, NY))
                send(src_of(*to), dst_of(dx, dy), dev(*to, c, z), out, into)
            sent(out, fifteen)
            yield
            arrive(into, fifteen)

        def halves(cut, rows):
            def split(ref, side):
                return ref.at[pl.ds(0, cut), :] if side == 0 else ref.at[pl.ds(cut, rows - cut), :]

            return split

        def rows_of(ref, start, size):
            return ref.at[pl.ds(pl.multiple_of(start, 16), size), :]

        yield from gather(
            "z", lambda at: b["g1"].at[at], halves(128, 256), b["g1"].at[0:7]
        )
        need("pinv")
        inner = jnp.dot(
            pinv_v[...], b["g1"][...].reshape(2048, w), preferred_element_type=F32
        )
        b["inner"][...] = inner
        b["g2"][z] = inner.astype(BF16)
        yield from gather(
            "z", lambda at: b["g2"].at[at], halves(128, 256), b["g2"].at[0:7]
        )
        need("coup")
        b["contrib"][...] = jnp.dot(
            coup_v[...], b["g2"][...].reshape(2048, w), preferred_element_type=F32
        ).reshape(6, BLK, w)
        local = [bmap[0, j] - z * 12 for j in range(6)]

        def placed(block):
            total = b["contrib"][0] * (local[0] == block).astype(F32)
            for j in range(1, 6):
                total = total + b["contrib"][j] * (local[j] == block).astype(F32)
            return total

        for j in range(6):
            b["s0"][j] = placed((1 - c) * 6 + j).astype(BF16)
        out = sem()
        swap = send(b["s0"], b["r0"], other, out, sem())
        sent(out, b["s0"])
        for j in range(6):
            b["dense"][j * BLK : (j + 1) * BLK, :] = placed(c * 6 + j)
        yield
        swap.wait_recv()
        b["dense"][...] = b["dense"][...] + b["r0"][...].reshape(768, w).astype(F32)
        b["sxy"][...] = b["dense"][...].astype(BF16)
        in_plane()
        mine = (x * NY + y) * PIECE
        yield from to_plane(
            lambda x_, y_: rows_of(b["sxy"], (x_ * NY + y_) * PIECE, PIECE),
            lambda dx, dy: b["rxy"].at[dx * NY + dy],
            b["rxy"].at[1:16],
        )
        total = rows_of(b["dense"], mine, PIECE)[...]
        for at in range(1, 16):
            total = total + b["rxy"][at].astype(F32)
        need("root")
        piece = rows_of(b["h"], c * 768 + mine, PIECE)
        piece[...] = (root_v[:, c0 : c0 + w] - total).astype(BF16)
        yield from to_plane(lambda x_, y_: piece, lambda dx, dy: piece, b["h"].at[0:720, :])
        mine = rows_of(b["h"], c * 768, 768)
        out = sem()
        swap = send(mine, mine, other, out, sem())
        sent(out, mine)
        need("rinv")

        def root_half(core):
            cols = pl.ds(pl.multiple_of(core * 768, 256), 768)
            return jnp.dot(
                rinv_v[:, cols], rows_of(b["h"], core * 768, 768)[...], preferred_element_type=F32
            )

        b["part"][...] = root_half(c)
        yield
        swap.wait_recv()
        part = b["part"][...] + root_half(1 - c)
        b["part"][...] = part
        b["parth"][...] = part.astype(BF16)
        out, into = sem(), sem()
        for s in (4, 3, 5, 2, 6, 1, 7):
            at = mod(z + s, NZ)
            src = rows_of(b["parth"], at * PIECE, PIECE)
            send(src, b["r5"].at[s], dev(x, y, c, at), out, into)
        sent(out, b["r5"].at[1:8])
        yield
        arrive(into, b["r5"].at[1:8])
        total = rows_of(b["part"], z * PIECE, PIECE)[...]
        for s in range(1, NZ):
            total = total + b["r5"][s].astype(F32)
        b["rout"][...] = total
        store(b["rout"], out_r.at[i])
        b["t"][...] = total.astype(BF16)
        out = sem()
        moved = send(b["t"], rows_of(b["k"], piece_out * PIECE, PIECE), perm_to, out, sem())
        sent(out, b["t"])
        yield
        moved.wait_recv()
        piece = rows_of(b["k"], piece_in * PIECE, PIECE)
        yield from to_plane(lambda x_, y_: piece, lambda dx, dy: piece, b["k"].at[0:720, :])
        out, into = sem(), sem()
        for g in range(2):
            mine = rows_of(b["k"], (g * 16 + core_from * 8) * PIECE, 8 * PIECE)
            send(mine, mine, other, out, into)
        sent(out, b["k"].at[0:768, :])
        yield
        arrive(into, b["k"].at[0:768, :])
        for j in range(6):
            total = b["k"][0:BLK, :] * (local[j] == 0).astype(F32).astype(BF16)
            for at in range(1, 12):
                mask = (local[j] == at).astype(F32).astype(BF16)
                total = total + b["k"][at * BLK : (at + 1) * BLK, :] * mask
            b["picked"][j * BLK : (j + 1) * BLK, :] = total
        pulled = lax.dot_general(
            b["picked"][...],
            coup_v[...],
            (((0,), (0,)), ((), ())),
            preferred_element_type=F32,
        )
        for at in range(NZ):
            b["q"][at] = pulled[:, at * 256 : (at + 1) * 256]
        total = yield from scatter(
            "z", lambda at: b["q"].at[at], w, w // 2, b["sp"], b["rp"], BF16, b["g3"].at[0:7]
        )
        b["g3"][z] = total.astype(BF16)
        yield from gather(
            "z", lambda at: b["g3"].at[at], halves(w // 2, w), b["g3"].at[0:7]
        )
        result = b["inner"][...]
        for at in range(NZ):
            result = result - lax.dot_general(
                pinv_v[:, at * 256 : (at + 1) * 256],
                b["g3"][at],
                (((1,), (1,)), ((), ())),
                preferred_element_type=F32,
            )
        b["fout"][...] = result
        store(b["fout"], out_f.at[i])

    live = [chunk(i, c0, w) for i, (c0, w) in enumerate(CHUNKS)] + [passes]
    while live:
        for gen in list(live):
            try:
                next(gen)
            except StopIteration:
                live.remove(gen)
    for out, ref in all_sent:
        pltpu.make_async_copy(ref, ref, out).wait()
    for copy in stores:
        copy.wait()


def join(f_ref, r_ref, out_f, out_r):
    for i, (c0, w) in enumerate(CHUNKS):
        out_f[:, c0 : c0 + w] = f_ref[i]
        out_r[:, c0 : c0 + w] = r_ref[i]


def per_device(*args):
    scratch = []
    for _, w in CHUNKS:
        scratch += list(scratch_for(w).values())
    scratch += [
        pltpu.VMEM((256, 384), BF16),
        pltpu.VMEM((256, 2048), BF16),
        pltpu.VMEM((768, 2048), BF16),
        pltpu.VMEM((384, 1536), BF16),
        pltpu.VMEM((PIECE, 384), F32),
        pltpu.SemaphoreType.DMA((len(CHUNKS), N_SEMS)),
        pltpu.SemaphoreType.DMA((8,)),
        pltpu.SemaphoreType.DMA((2 * len(CHUNKS),)),
        pltpu.SemaphoreType.REGULAR((3,)),
    ]
    hbm = pl.BlockSpec(memory_space=pl.ANY)
    vmem = pl.BlockSpec(memory_space=pltpu.VMEM)
    n, w = len(CHUNKS), CHUNKS[0][1]
    parts = pl.pallas_call(
        kernel,
        out_shape=(
            jax.ShapeDtypeStruct((n, 256, w), F32),
            jax.ShapeDtypeStruct((n, PIECE, w), F32),
        ),
        in_specs=[hbm] * 5 + [pl.BlockSpec(memory_space=pltpu.SMEM)],
        out_specs=(hbm, hbm),
        scratch_shapes=scratch,
        compiler_params=pltpu.CompilerParams(
            collective_id=0, has_side_effects=True, vmem_limit_bytes=60 * 2**20
        ),
        name="solve",
    )(*args)
    return pl.pallas_call(
        join,
        out_shape=(
            jax.ShapeDtypeStruct((256, 384), F32),
            jax.ShapeDtypeStruct((PIECE, 384), F32),
        ),
        in_specs=[vmem, vmem],
        out_specs=(vmem, vmem),
        name="join",
    )(*parts)


def solution(mesh):
    in_specs = (
        P(("front", "row"), None),
        P("row", None),
        P(("front", "row"), None),
        P(("front", "row"), None),
        P("front", "row"),
        P("front", "row"),
    )
    out_specs = (P(("front", "row"), None), P(("front", "row"), None))
    return jax.shard_map(
        per_device, mesh=mesh, in_specs=in_specs, out_specs=out_specs, check_vma=False
    )
```

time: 134 us -> 123 us (0.918)
  Pallas kernels: 130 us -> 121 us
  local copies, waits for them, and re-layouts: 3.29 us -> 0 us
    pallas_call x1 -> x2, Pallas kernels: 130 us -> 121 us  [the longest x1 119 us: per_device(): pl.pallas_call(kernel, out_shape=(jax.ShapeDtypeStruct((n, 256, w), F32),...]
    unnamed x2 -> x0, local copies, waits for them, and re-layouts: 3.29 us -> none
where the time goes in v3:
time: 123 us; the launch traced here: 121 us
  Pallas kernels  121 us (98%)
    pallas_call x1, Pallas kernels, per_device(): pl.pallas_call(kernel, out_shape=(jax.ShapeDtypeStruct((n, 256, w), F32),...  119 us

profile of v3, /device:TPU:2, one launch (start us, length us, event | category | flops | bytes accessed | tf_op | source)
XLA Modules:
  0.0 121.5 jit_solution(15585381036435623513)
XLA Ops:
  0.6 119.0 %solve.1 = (f32[3,256,128]{2,1,0:T(8,128)}, f32[3,48,128]{2,1,0:T(8,128)}) custom-call(bf16[256,384]{1,0:T(8,128)(2,1)} %rhs.1, f32[1536,384]{1,0:T(8,128)} %rroot.1, bf16[256,2048]{1,0:T(8,128)(2,1)} %pinv.1, bf16[768,2048]{1,0:T(8,128)(2,1)} %coup.1, bf16[384,1536]{1,0:T(8,128)(2,1)} %rinv.1, s32[1,6]{1,0:T(1,128)} %bmap.1), custom_call_target="tpu_custom_call" | custom-call | tf_op jit(solution)/shard_map/solve/pallas_call | solution.py:431
  119.7 1.8 %join.1 = (f32[256,384]{1,0:T(8,128)}, f32[48,384]{1,0:T(8,128)}) custom-call(f32[3,256,128]{2,1,0:T(8,128)} %get-tuple-element.4.f_ref, f32[3,48,128]{2,1,0:T(8,128)} %get-tuple-element.5.r_ref), custom_call_target="tpu_custom_call" | custom-call | tf_op jit(solution)/shard_map/join/pallas_call | solution.py:445

commit v4 on v3

--- a/solution.py
+++ b/solution.py
@@ -17,6 +17,7 @@
     key=lambda o: -(min(o[0], NX - o[0]) + min(o[1], NY - o[1])),
 )
 N_SEMS = 28
+DELAYS = (0, 0, 1)
 
 
 def scratch_for(w):
@@ -25,7 +26,7 @@
         g1=v((NZ, 256, w), BF16),
         inner=v((256, w), F32),
         g2=v((NZ, 256, w), BF16),
-        contrib=v((6, BLK, w), F32),
+        contrib=v((768, w), F32),
         s0=v((6, BLK, w), BF16),
         r0=v((6, BLK, w), BF16),
         dense=v((768, w), F32),
@@ -38,12 +39,11 @@
         t=v((PIECE, w), BF16),
         k=v((1536, w), BF16),
         picked=v((768, w), BF16),
+        turned=v((w, 768), BF16),
         q=v((NZ, w, 256), F32),
         sp=v((2, 4, w, 256), BF16),
         rp=v((2, 4, w, 256), BF16),
         g3=v((NZ, w, 256), BF16),
-        rout=v((PIECE, w), F32),
-        fout=v((256, w), F32),
     )
 
 
@@ -59,7 +59,7 @@
     bufs = [
         dict(zip(NAMES, scratch[i * per : (i + 1) * per])) for i in range(len(CHUNKS))
     ]
-    rhs_v, pinv_v, coup_v, rinv_v, root_v, sems, load_sems, store_sems, pass_sems = scratch[per * len(CHUNKS) :]
+    rhs_v, pinv_v, coup_v, rinv_v, root_v, sems, load_sems, pass_sems = scratch[per * len(CHUNKS) :]
 
     f = lax.axis_index("front")
     z = lax.axis_index("row")
@@ -135,14 +135,6 @@
 
     passes = passing()
     all_sent = []
-    stores = []
-
-    def store(src, dst):
-        copy = pltpu.make_async_copy(src, dst, store_sems.at[len(stores)])
-        copy.start()
-        stores.append(copy)
-
-
     def in_plane():
         for _ in passes:
             pass
@@ -177,7 +169,7 @@
         def arrive(into, ref):
             pltpu.make_async_copy(ref, ref, into).wait()
 
-        def gather(axis, slot, split, seven):
+        def gather(axis, slot, split, seven, seen):
             n, me, plus, minus = rings[axis]
             half = n // 2
             out = sem()
@@ -185,6 +177,7 @@
             ups, downs = ring_sems
             a = send(slot(me), slot(me), plus, out, ups[0])
             d = send(slot(me), slot(me), minus, out, downs[0])
+            seen(me)
             for s in range(1, half):
                 yield
                 a.wait_recv()
@@ -197,13 +190,17 @@
                 if s == half - 1:
                     got = split(got, 1)
                 d = send(got, got, minus, out, downs[s])
+                seen(mod(me - s, n))
+                seen(mod(me + s, n))
             yield
             a.wait_recv()
             d.wait_recv()
-
-        def scatter(axis, own, rows, cut, sbuf, rbuf, wire, seven):
+            seen(mod(me + half, n))
+
+        def scatter(axis, own, make, rows, cut, sbuf, rbuf, wire, seven):
             n, me, plus, minus = rings[axis]
             half = n // 2
+            make(mod(me + half, n))
             far = own(mod(me + half, n))
             sides = ((slice(0, cut), plus), (slice(cut, rows), minus))
             copies = []
@@ -221,6 +218,8 @@
                     )
                 )
             for s in range(1, half):
+                make(mod(me + half - s, n))
+                make(mod(me - half + s, n))
                 yield
                 for side, (span, to) in enumerate(sides):
                     copies[side].wait_recv()
@@ -237,6 +236,7 @@
                     copies[side] = send(
                         sbuf.at[side, s], rbuf.at[side, s], to, out, ring_sems[side][s]
                     )
+            make(me)
             yield
             copies[0].wait_recv()
             copies[1].wait_recv()
@@ -264,28 +264,35 @@
         def rows_of(ref, start, size):
             return ref.at[pl.ds(pl.multiple_of(start, 16), size), :]
 
+        def cols(ref, at):
+            return ref[:, pl.ds(pl.multiple_of(at * 256, 256), 256)]
+
+        def summing(acc, weights, pieces, name):
+            first = [True]
+
+            def seen(at):
+                need(name)
+                term = jnp.dot(cols(weights, at), pieces[at], preferred_element_type=F32)
+                acc[...] = term if first[0] else acc[...] + term
+                first[0] = False
+
+            return seen
+
         yield from gather(
-            "z", lambda at: b["g1"].at[at], halves(128, 256), b["g1"].at[0:7]
-        )
-        need("pinv")
-        inner = jnp.dot(
-            pinv_v[...], b["g1"][...].reshape(2048, w), preferred_element_type=F32
-        )
-        b["inner"][...] = inner
-        b["g2"][z] = inner.astype(BF16)
+            "z", lambda at: b["g1"].at[at], halves(128, 256), b["g1"].at[0:7],
+            summing(b["inner"], pinv_v, b["g1"], "pinv"),
+        )
+        b["g2"][z] = b["inner"][...].astype(BF16)
         yield from gather(
-            "z", lambda at: b["g2"].at[at], halves(128, 256), b["g2"].at[0:7]
-        )
-        need("coup")
-        b["contrib"][...] = jnp.dot(
-            coup_v[...], b["g2"][...].reshape(2048, w), preferred_element_type=F32
-        ).reshape(6, BLK, w)
+            "z", lambda at: b["g2"].at[at], halves(128, 256), b["g2"].at[0:7],
+            summing(b["contrib"], coup_v, b["g2"], "coup"),
+        )
         local = [bmap[0, j] - z * 12 for j in range(6)]
 
         def placed(block):
-            total = b["contrib"][0] * (local[0] == block).astype(F32)
+            total = b["contrib"][0:BLK, :] * (local[0] == block).astype(F32)
             for j in range(1, 6):
-                total = total + b["contrib"][j] * (local[j] == block).astype(F32)
+                total = total + b["contrib"][j * BLK : (j + 1) * BLK, :] * (local[j] == block).astype(F32)
             return total
 
         for j in range(6):
@@ -342,8 +349,7 @@
         total = rows_of(b["part"], z * PIECE, PIECE)[...]
         for s in range(1, NZ):
             total = total + b["r5"][s].astype(F32)
-        b["rout"][...] = total
-        store(b["rout"], out_r.at[i])
+        out_r[i] = total
         b["t"][...] = total.astype(BF16)
         out = sem()
         moved = send(b["t"], rows_of(b["k"], piece_out * PIECE, PIECE), perm_to, out, sem())
@@ -365,43 +371,43 @@
                 mask = (local[j] == at).astype(F32).astype(BF16)
                 total = total + b["k"][at * BLK : (at + 1) * BLK, :] * mask
             b["picked"][j * BLK : (j + 1) * BLK, :] = total
-        pulled = lax.dot_general(
-            b["picked"][...],
-            coup_v[...],
-            (((0,), (0,)), ((), ())),
-            preferred_element_type=F32,
-        )
-        for at in range(NZ):
-            b["q"][at] = pulled[:, at * 256 : (at + 1) * 256]
+        b["turned"][...] = b["picked"][...].T
+
+        def pull(at):
+            b["q"][at] = jnp.dot(b["turned"][...], cols(coup_v, at), preferred_element_type=F32)
+
         total = yield from scatter(
-            "z", lambda at: b["q"].at[at], w, w // 2, b["sp"], b["rp"], BF16, b["g3"].at[0:7]
+            "z", lambda at: b["q"].at[at], pull, w, w // 2, b["sp"], b["rp"], BF16, b["g3"].at[0:7]
         )
         b["g3"][z] = total.astype(BF16)
-        yield from gather(
-            "z", lambda at: b["g3"].at[at], halves(w // 2, w), b["g3"].at[0:7]
-        )
-        result = b["inner"][...]
-        for at in range(NZ):
-            result = result - lax.dot_general(
-                pinv_v[:, at * 256 : (at + 1) * 256],
+        out_f_i = out_f.at[i]
+        out_f_i[...] = b["inner"][...]
+
+        def correct(at):
+            out_f_i[...] = out_f_i[...] - lax.dot_general(
+                cols(pinv_v, at),
                 b["g3"][at],
                 (((1,), (1,)), ((), ())),
                 preferred_element_type=F32,
             )
-        b["fout"][...] = result
-        store(b["fout"], out_f.at[i])
+
+        yield from gather(
+            "z", lambda at: b["g3"].at[at], halves(w // 2, w), b["g3"].at[0:7], correct
+        )
 
     live = [chunk(i, c0, w) for i, (c0, w) in enumerate(CHUNKS)] + [passes]
+    wait = dict(zip(live, DELAYS))
     while live:
         for gen in list(live):
+            if wait.get(gen, 0):
+                wait[gen] -= 1
+                continue
             try:
                 next(gen)
             except StopIteration:
                 live.remove(gen)
     for out, ref in all_sent:
         pltpu.make_async_copy(ref, ref, out).wait()
-    for copy in stores:
-        copy.wait()
 
 
 def join(f_ref, r_ref, out_f, out_r):
@@ -422,7 +428,6 @@
         pltpu.VMEM((PIECE, 384), F32),
         pltpu.SemaphoreType.DMA((len(CHUNKS), N_SEMS)),
         pltpu.SemaphoreType.DMA((8,)),
-        pltpu.SemaphoreType.DMA((2 * len(CHUNKS),)),
         pltpu.SemaphoreType.REGULAR((3,)),
     ]
     hbm = pl.BlockSpec(memory_space=pl.ANY)
@@ -431,11 +436,11 @@
     parts = pl.pallas_call(
         kernel,
         out_shape=(
-            jax.ShapeDtypeStruct((n, 256, w), F32),
-            jax.ShapeDtypeStruct((n, PIECE, w), F32),
+            pltpu.VMEM((n, 256, w), F32),
+            pltpu.VMEM((n, PIECE, w), F32),
         ),
         in_specs=[hbm] * 5 + [pl.BlockSpec(memory_space=pltpu.SMEM)],
-        out_specs=(hbm, hbm),
+        out_specs=(vmem, vmem),
         scratch_shapes=scratch,
         compiler_params=pltpu.CompilerParams(
             collective_id=0, has_side_effects=True, vmem_limit_bytes=60 * 2**20
@@ -451,7 +456,7 @@
         in_specs=[vmem, vmem],
         out_specs=(vmem, vmem),
         name="join",
-    )(*parts)
+    )(*[pltpu.with_memory_space_constraint(part, pltpu.VMEM) for part in parts])
 
 
 def solution(mesh):

time: 123 us -> 117 us (0.951)
  Pallas kernels: 121 us -> 115 us
    pallas_call x1, Pallas kernels: 119 us -> 114 us  [per_device(): pl.pallas_call(kernel, out_shape=(pltpu.VMEM((n, 256, w), F32), pltpu.VME...]
where the time goes in v4:
time: 117 us; the launch traced here: 116 us
  Pallas kernels  115 us (98%)
    pallas_call x1, Pallas kernels, per_device(): pl.pallas_call(kernel, out_shape=(pltpu.VMEM((n, 256, w), F32), pltpu.VME...  114 us

profile of v4, /device:TPU:2, one launch (start us, length us, event | category | flops | bytes accessed | tf_op | source)
XLA Modules:
  0.0 115.8 jit_solution(12449115693193254592)
XLA Ops:
  0.6 114.4 %solve.1 = (f32[3,256,128]{2,1,0:T(8,128)S(1)}, f32[3,48,128]{2,1,0:T(8,128)S(1)}) custom-call(bf16[256,384]{1,0:T(8,128)(2,1)} %rhs.1, f32[1536,384]{1,0:T(8,128)} %rroot.1, bf16[256,2048]{1,0:T(8,128)(2,1)} %pinv.1, bf16[768,2048]{1,0:T(8,128)(2,1)} %coup.1, bf16[384,1536]{1,0:T(8,128)(2,1)} %rinv.1, s32[1,6]{1,0:T(1,128)} %bmap.1), custom_call_target="tpu_custom_call" | custom-call | tf_op jit(solution)/shard_map/solve/pallas_call | solution.py:436
  115.1 0.8 join.1

commit v5 on v4

--- a/solution.py
+++ b/solution.py
@@ -27,6 +27,7 @@
         inner=v((256, w), F32),
         g2=v((NZ, 256, w), BF16),
         contrib=v((768, w), F32),
+        rounded=v((768, w), BF16),
         s0=v((6, BLK, w), BF16),
         r0=v((6, BLK, w), BF16),
         dense=v((768, w), F32),
@@ -59,7 +60,7 @@
     bufs = [
         dict(zip(NAMES, scratch[i * per : (i + 1) * per])) for i in range(len(CHUNKS))
     ]
-    rhs_v, pinv_v, coup_v, rinv_v, root_v, sems, load_sems, pass_sems = scratch[per * len(CHUNKS) :]
+    rhs_v, pinv_v, coup_v, rinv_v, root_v, bmap_s, sems, load_sems, pass_sems = scratch[per * len(CHUNKS) :]
 
     f = lax.axis_index("front")
     z = lax.axis_index("row")
@@ -118,6 +119,7 @@
     load("coup", coup, coup_v)
     load("root", rroot.at[pl.ds(piece_row, PIECE), :], root_v)
     load("rinv", rinv, rinv_v)
+    load("bmap", bmap, bmap_s)
     need("rhs")
     for i, (c0, w) in enumerate(CHUNKS):
         bufs[i]["g1"][z] = rhs_v[:, c0 : c0 + w]
@@ -177,9 +179,11 @@
             ups, downs = ring_sems
             a = send(slot(me), slot(me), plus, out, ups[0])
             d = send(slot(me), slot(me), minus, out, downs[0])
-            seen(me)
+            pieces = [me]
             for s in range(1, half):
                 yield
+                for at in pieces:
+                    seen(at)
                 a.wait_recv()
                 got = slot(mod(me - s, n))
                 if s == half - 1:
@@ -190,9 +194,10 @@
                 if s == half - 1:
                     got = split(got, 1)
                 d = send(got, got, minus, out, downs[s])
-                seen(mod(me - s, n))
-                seen(mod(me + s, n))
+                pieces = [mod(me - s, n), mod(me + s, n)]
             yield
+            for at in pieces:
+                seen(at)
             a.wait_recv()
             d.wait_recv()
             seen(mod(me + half, n))
@@ -218,9 +223,9 @@
                     )
                 )
             for s in range(1, half):
+                yield
                 make(mod(me + half - s, n))
                 make(mod(me - half + s, n))
-                yield
                 for side, (span, to) in enumerate(sides):
                     copies[side].wait_recv()
                     at = mod(me + half - s, n) if side == 0 else mod(me - half + s, n)
@@ -236,8 +241,8 @@
                     copies[side] = send(
                         sbuf.at[side, s], rbuf.at[side, s], to, out, ring_sems[side][s]
                     )
+            yield
             make(me)
-            yield
             copies[0].wait_recv()
             copies[1].wait_recv()
             return (
@@ -287,21 +292,25 @@
             "z", lambda at: b["g2"].at[at], halves(128, 256), b["g2"].at[0:7],
             summing(b["contrib"], coup_v, b["g2"], "coup"),
         )
-        local = [bmap[0, j] - z * 12 for j in range(6)]
-
-        def placed(block):
-            total = b["contrib"][0:BLK, :] * (local[0] == block).astype(F32)
-            for j in range(1, 6):
-                total = total + b["contrib"][j * BLK : (j + 1) * BLK, :] * (local[j] == block).astype(F32)
+        need("bmap")
+        local = [bmap_s[0, j] - z * 12 for j in range(6)]
+
+        def placed(block, name, kind):
+            total = None
+            for j in range(6):
+                term = b[name][j * BLK : (j + 1) * BLK, :] * (local[j] == block).astype(F32).astype(kind)
+                total = term if total is None else total + term
             return total
 
+        b["rounded"][...] = b["contrib"][...].astype(BF16)
+
         for j in range(6):
-            b["s0"][j] = placed((1 - c) * 6 + j).astype(BF16)
+            b["s0"][j] = placed((1 - c) * 6 + j, "rounded", BF16)
         out = sem()
         swap = send(b["s0"], b["r0"], other, out, sem())
         sent(out, b["s0"])
         for j in range(6):
-            b["dense"][j * BLK : (j + 1) * BLK, :] = placed(c * 6 + j)
+            b["dense"][j * BLK : (j + 1) * BLK, :] = placed(c * 6 + j, "contrib", F32)
         yield
         swap.wait_recv()
         b["dense"][...] = b["dense"][...] + b["r0"][...].reshape(768, w).astype(F32)
@@ -426,6 +435,7 @@
         pltpu.VMEM((768, 2048), BF16),
         pltpu.VMEM((384, 1536), BF16),
         pltpu.VMEM((PIECE, 384), F32),
+        pltpu.SMEM((1, 6), jnp.int32),
         pltpu.SemaphoreType.DMA((len(CHUNKS), N_SEMS)),
         pltpu.SemaphoreType.DMA((8,)),
         pltpu.SemaphoreType.REGULAR((3,)),
@@ -439,7 +449,7 @@
             pltpu.VMEM((n, 256, w), F32),
             pltpu.VMEM((n, PIECE, w), F32),
         ),
-        in_specs=[hbm] * 5 + [pl.BlockSpec(memory_space=pltpu.SMEM)],
+        in_specs=[hbm] * 6,
         out_specs=(vmem, vmem),
         scratch_shapes=scratch,
         compiler_params=pltpu.CompilerParams(

time: 117 us -> 116 us (level)
  no operation moved by 1% of the time
where the time goes in v5:
time: 116 us
  Pallas kernels  115 us (99%)
    pallas_call x1, Pallas kernels, per_device(): pl.pallas_call(kernel, out_shape=(pltpu.VMEM((n, 256, w), F32), pltpu.VME...  114 us

profile of v5, /device:TPU:2, one launch (start us, length us, event | category | flops | bytes accessed | tf_op | source)
XLA Modules:
  0.0 115.8 jit_solution(6233856739014160553)
XLA Ops:
  0.6 114.4 %solve.1 = (f32[3,256,128]{2,1,0:T(8,128)S(1)}, f32[3,48,128]{2,1,0:T(8,128)S(1)}) custom-call(bf16[256,384]{1,0:T(8,128)(2,1)} %rhs.1, f32[1536,384]{1,0:T(8,128)} %rroot.1, bf16[256,2048]{1,0:T(8,128)(2,1)} %pinv.1, bf16[768,2048]{1,0:T(8,128)(2,1)} %coup.1, bf16[384,1536]{1,0:T(8,128)(2,1)} %rinv.1, s32[1,6]{1,0:T(1,128)} %bmap.1), custom_call_target="tpu_custom_call" | custom-call | tf_op jit(solution)/shard_map/solve/pallas_call | solution.py:446
  115.0 0.8 join.1

commit v6 on v5

--- a/solution.py
+++ b/solution.py
@@ -121,8 +121,6 @@
     load("rinv", rinv, rinv_v)
     load("bmap", bmap, bmap_s)
     need("rhs")
-    for i, (c0, w) in enumerate(CHUNKS):
-        bufs[i]["g1"][z] = rhs_v[:, c0 : c0 + w]
     pl.semaphore_wait(barrier, len(partners))
 
     def passing():
@@ -269,6 +267,8 @@
         def rows_of(ref, start, size):
             return ref.at[pl.ds(pl.multiple_of(start, 16), size), :]
 
+        b["g1"][z] = rhs_v[:, c0 : c0 + w]
+
         def cols(ref, at):
             return ref[:, pl.ds(pl.multiple_of(at * 256, 256), 256)]
 

time: 116 us -> 116 us (level)
  no operation moved by 1% of the time
where the time goes in v6:
time: 116 us
  Pallas kernels  115 us (99%)
    pallas_call x1, Pallas kernels, per_device(): pl.pallas_call(kernel, out_shape=(pltpu.VMEM((n, 256, w), F32), pltpu.VME...  114 us

profile of v6, /device:TPU:2, one launch (start us, length us, event | category | flops | bytes accessed | tf_op | source)
XLA Modules:
  0.0 115.8 jit_solution(17182640804073691742)
XLA Ops:
  0.6 114.3 %solve.1 = (f32[3,256,128]{2,1,0:T(8,128)S(1)}, f32[3,48,128]{2,1,0:T(8,128)S(1)}) custom-call(bf16[256,384]{1,0:T(8,128)(2,1)} %rhs.1, f32[1536,384]{1,0:T(8,128)} %rroot.1, bf16[256,2048]{1,0:T(8,128)(2,1)} %pinv.1, bf16[768,2048]{1,0:T(8,128)(2,1)} %coup.1, bf16[384,1536]{1,0:T(8,128)(2,1)} %rinv.1, s32[1,6]{1,0:T(1,128)} %bmap.1), custom_call_target="tpu_custom_call" | custom-call | tf_op jit(solution)/shard_map/solve/pallas_call | solution.py:446
  115.0 0.8 join.1
